TPU v7x, 32 devices: a whole 2x2x4 slice. The times are simulated.
32 devices in a mesh: replica: 16 (over z, x, core), shard: 2 (over y).
Axes of the slice: x: 2, y: 2, z: 4, core: 2. Of those that a mesh axis runs over, the one named last changes fastest.
Arguments:
- latents: bfloat16 [32, 1024, 1152], P('replica', 'shard'), may hold values from -6 to 6
- conditions: bfloat16 [32, 1152], P('replica'), may hold values from -6 to 6
- cotangent: bfloat16 [32, 1024, 1152], P('replica', 'shard'), may hold values from -6 to 6
- counts: int32 [16], P('replica'), may hold values from 1 to 2, as said below
- w_ada: bfloat16 [1152, 6912], P('shard'), may hold values from -0.1875 to 0.1875
- b_ada: bfloat16 [6912], P('shard'), may hold values from -3 to 3
- w_qkv: bfloat16 [1152, 3456], P('shard'), may hold values from -0.1875 to 0.1875
- b_qv: bfloat16 [2304], P('shard'), may hold values from -3 to 3
- w_proj: bfloat16 [1152, 1152], P('shard'), may hold values from -3.5 to 3.5
- b_proj: bfloat16 [1152], P('shard'), may hold values from -3 to 3
- w_fc1: bfloat16 [1152, 4608], P('shard'), may hold values from -0.1875 to 0.1875
- b_fc1: bfloat16 [4608], P('shard'), may hold values from -3 to 3
- w_fc2: bfloat16 [4608, 1152], P('shard'), may hold values from -0.09375 to 0.09375
- b_fc2: bfloat16 [1152], P('shard'), may hold values from -3 to 3
Outputs:
- output: bfloat16 [32, 1024, 1152], P('replica', 'shard')
- grad_latents: float32 [32, 1024, 1152], P('replica', 'shard')
- grad_conditions: float32 [32, 1152], P('replica')
- grad_w_ada: float32 [1152, 6912], P('shard')
- grad_b_ada: float32 [6912], P('shard')
- grad_w_qkv: float32 [1152, 3456], P('shard')
- grad_b_qv: float32 [2304], P('shard')
- grad_w_proj: float32 [1152, 1152], P('shard')
- grad_b_proj: float32 [1152], P('shard')
- grad_w_fc1: float32 [1152, 4608], P('shard')
- grad_b_fc1: float32 [4608], P('shard')
- grad_w_fc2: float32 [4608, 1152], P('shard')
- grad_b_fc2: float32 [1152], P('shard')
Inputs may be any that keep to these rules, and one draw needn't show every extreme that they name: counts[r] live slots on replica r are its slots 0 to counts[r] - 1 of 2; some replica has all 2 live.
All inputs are finite; a program needn't handle non-finite values.
Results may differ from a plain program's by a relative error of at most 0.019.
Values may be sent and summed in bfloat16 or wider, within the bound.
A program may use at most 512 MiB of HBM per device.

v0:
```python
from functools import partial
import math
import jax
import jax.numpy as jnp
from jax import lax
from jax.sharding import PartitionSpec as P

HEADS = 16
HDIM = 72
epsilon = 1e-06


def layer_stats(values):
    centered = values - jnp.mean(values, axis=-1, keepdims=True)
    inverse = lax.rsqrt(jnp.mean(centered * centered, axis=-1, keepdims=True) + epsilon)
    return (centered * inverse, inverse)


def layer_back(normal, inverse, d_normal):
    first_mean = jnp.mean(d_normal, axis=-1, keepdims=True)
    second_mean = jnp.mean(d_normal * normal, axis=-1, keepdims=True)
    return inverse * (d_normal - first_mean - normal * second_mean)


def contract_last(left, right):
    return lax.dot_general(
        left, right, (((1,), (1,)), ((), ())), preferred_element_type=jnp.float32
    )


def forward_product(inputs, whole_pair):
    return (
        jnp.dot(inputs, whole_pair[0], preferred_element_type=jnp.float32),
        whole_pair[1].astype(jnp.float32),
    )


def backward_product(grads, whole_pair):
    return contract_last(grads, whole_pair[0])


def owner_grads(inputs, grads, weight_rows, bias_terms):
    columns = lax.slice_in_dim(inputs, 0, weight_rows * lax.axis_size("shard"), axis=1)
    weight_grad = lax.psum_scatter(
        lax.dot_general(
            columns, grads, (((0,), (0,)), ((), ())), preferred_element_type=jnp.float32
        ).astype(jnp.bfloat16),
        "shard",
        scatter_dimension=0,
        tiled=True,
    ).astype(jnp.float32)
    bias_grad = lax.psum_scatter(
        bias_terms.astype(jnp.bfloat16), "shard", scatter_dimension=0, tiled=True
    ).astype(jnp.float32)
    return (weight_grad, bias_grad)


def shards(
    latents,
    conditions,
    cotangent,
    counts,
    w_ada,
    b_ada,
    w_qkv,
    b_qv,
    w_proj,
    b_proj,
    w_fc1,
    b_fc1,
    w_fc2,
    b_fc2,
):
    slots, block, width = latents.shape
    n_rows = slots * block
    scale = 1.0 / math.sqrt(HDIM)
    live = (jnp.arange(slots, dtype=jnp.int32) < counts[0]).astype(jnp.float32)[:, None, None]
    gathered = (
        lax.all_gather(w_ada, "shard", axis=0, tiled=True),
        lax.all_gather(b_ada, "shard", axis=0, tiled=True),
        lax.all_gather(w_qkv, "shard", axis=0, tiled=True),
        lax.all_gather(b_qv, "shard", axis=0, tiled=True),
        lax.all_gather(w_proj, "shard", axis=0, tiled=True),
        lax.all_gather(b_proj, "shard", axis=0, tiled=True),
        lax.all_gather(w_fc1, "shard", axis=0, tiled=True),
        lax.all_gather(b_fc1, "shard", axis=0, tiled=True),
        lax.all_gather(w_fc2, "shard", axis=0, tiled=True),
        lax.all_gather(b_fc2, "shard", axis=0, tiled=True),
    )
    full_ada = (gathered[0], gathered[1])
    full_qkv = (gathered[2], gathered[3])
    full_proj = (gathered[4], gathered[5])
    full_fc1 = (gathered[6], gathered[7])
    full_fc2 = (gathered[8], gathered[9])
    cond_float = conditions.astype(jnp.float32)
    cond_act = jax.nn.silu(cond_float).astype(jnp.bfloat16)
    ada_prod, ada_bias = forward_product(cond_act, full_ada)
    modul = ada_prod + ada_bias
    shift_a, scale_a, gate_a, shift_m, scale_m, gate_m = [
        piece[:, None, :] for piece in jnp.split(modul, 6, axis=1)
    ]
    tokens = latents.astype(jnp.float32)
    norm_a, inv_a = layer_stats(tokens)
    normed = (norm_a * (1.0 + scale_a) + shift_a).astype(jnp.bfloat16).reshape(n_rows, width)
    qkv_prod, qv_bias = forward_product(normed, full_qkv)
    query = (
        (qkv_prod[:, :width] + qv_bias[:width])
        .astype(jnp.bfloat16)
        .reshape(slots, block, HEADS, HDIM)
    )
    keys_own = qkv_prod[:, width : 2 * width].astype(jnp.bfloat16).reshape(slots, block, width)
    values_own = (
        (qkv_prod[:, 2 * width :] + qv_bias[width:])
        .astype(jnp.bfloat16)
        .reshape(slots, block, width)
    )
    keys_all, values_all = (
        lax.all_gather(keys_own, "shard", axis=1, tiled=True),
        lax.all_gather(values_own, "shard", axis=1, tiled=True),
    )
    length = keys_all.shape[1]
    keys_h = keys_all.reshape(slots, length, HEADS, HDIM)
    values_h = values_all.reshape(slots, length, HEADS, HDIM)
    scores = (
        jnp.einsum("sqhd,skhd->shqk", query, keys_h, preferred_element_type=jnp.float32) * scale
    )
    top_score = jnp.max(scores, axis=-1, keepdims=True)
    log_total = top_score + jnp.log(jnp.sum(jnp.exp(scores - top_score), axis=-1, keepdims=True))
    probs_low = jnp.exp(scores - log_total).astype(jnp.bfloat16)
    attended = jnp.einsum(
        "shqk,skhd->sqhd", probs_low, values_h, preferred_element_type=jnp.float32
    )
    attended = attended.astype(jnp.bfloat16).reshape(n_rows, width)
    proj_prod, proj_bias = forward_product(attended, full_proj)
    branch_a = (proj_prod + proj_bias).reshape(slots, block, width)
    resid = tokens + gate_a * branch_a
    norm_m, inv_m = layer_stats(resid)
    mixed = (norm_m * (1.0 + scale_m) + shift_m).astype(jnp.bfloat16).reshape(n_rows, width)
    fc1_prod, fc1_bias = forward_product(mixed, full_fc1)
    activated, gelu_back = jax.vjp(partial(jax.nn.gelu, approximate=True), fc1_prod + fc1_bias)
    hidden = activated.astype(jnp.bfloat16)
    fc2_prod, fc2_bias = forward_product(hidden, full_fc2)
    branch_m = (fc2_prod + fc2_bias).reshape(slots, block, width)
    final = resid + gate_m * branch_m
    output = (final * live).astype(jnp.bfloat16)
    d_out = cotangent.astype(jnp.float32) * live
    d_gate_m = jnp.sum(d_out * branch_m, axis=1)
    d_branch_m = (gate_m * d_out).astype(jnp.bfloat16).reshape(n_rows, width)
    pair_fc2 = owner_grads(
        hidden, d_branch_m, w_fc2.shape[0], jnp.sum(d_branch_m, axis=0, dtype=jnp.float32)
    )
    d_hidden = backward_product(d_branch_m, full_fc2)
    d_pre = gelu_back(d_hidden)[0].astype(jnp.bfloat16)
    pair_fc1 = owner_grads(mixed, d_pre, w_fc1.shape[0], jnp.sum(d_pre, axis=0, dtype=jnp.float32))
    d_mixed = backward_product(d_pre, full_fc1).reshape(slots, block, width)
    d_shift_m = jnp.sum(d_mixed, axis=1)
    d_scale_m = jnp.sum(d_mixed * norm_m, axis=1)
    d_resid = d_out + layer_back(norm_m, inv_m, d_mixed * (1.0 + scale_m))
    d_gate_a = jnp.sum(d_resid * branch_a, axis=1)
    d_branch_a = (gate_a * d_resid).astype(jnp.bfloat16).reshape(n_rows, width)
    pair_proj = owner_grads(
        attended, d_branch_a, w_proj.shape[0], jnp.sum(d_branch_a, axis=0, dtype=jnp.float32)
    )
    d_attended = (
        backward_product(d_branch_a, full_proj)
        .astype(jnp.bfloat16)
        .reshape(slots, block, HEADS, HDIM)
    )
    scores = (
        jnp.einsum("sqhd,skhd->shqk", query, keys_h, preferred_element_type=jnp.float32) * scale
    )
    probs = jnp.exp(scores - log_total)
    d_probs = jnp.einsum(
        "sqhd,skhd->shqk", d_attended, values_h, preferred_element_type=jnp.float32
    )
    inner = jnp.sum(d_probs * probs, axis=-1, keepdims=True)
    d_scores = (probs * (d_probs - inner)).astype(jnp.bfloat16)
    d_query = (
        (
            jnp.einsum("shqk,skhd->sqhd", d_scores, keys_h, preferred_element_type=jnp.float32)
            * scale
        )
        .astype(jnp.bfloat16)
        .reshape(n_rows, width)
    )
    key_terms = (
        jnp.einsum("shqk,sqhd->skhd", d_scores, query, preferred_element_type=jnp.float32).reshape(
            slots, length, width
        )
        * scale
    )
    value_terms = jnp.einsum(
        "shqk,sqhd->skhd",
        probs.astype(jnp.bfloat16),
        d_attended,
        preferred_element_type=jnp.float32,
    ).reshape(slots, length, width)
    d_keys, d_values = (
        lax.psum_scatter(
            key_terms.astype(jnp.bfloat16), "shard", scatter_dimension=1, tiled=True
        ).astype(jnp.float32),
        lax.psum_scatter(
            value_terms.astype(jnp.bfloat16), "shard", scatter_dimension=1, tiled=True
        ).astype(jnp.float32),
    )
    d_keys = d_keys.astype(jnp.bfloat16).reshape(n_rows, width)
    d_values = d_values.astype(jnp.bfloat16).reshape(n_rows, width)
    d_qkv = jnp.concatenate([d_query, d_keys, d_values], axis=1)
    qv_terms = jnp.concatenate(
        [jnp.sum(d_query, axis=0, dtype=jnp.float32), jnp.sum(d_values, axis=0, dtype=jnp.float32)]
    )
    pair_qkv = owner_grads(normed, d_qkv, w_qkv.shape[0], qv_terms)
    d_normed = backward_product(d_qkv, full_qkv).reshape(slots, block, width)
    d_shift_a = jnp.sum(d_normed, axis=1)
    d_scale_a = jnp.sum(d_normed * norm_a, axis=1)
    grad_latents = d_resid + layer_back(norm_a, inv_a, d_normed * (1.0 + scale_a))
    d_modul_part = jnp.concatenate(
        [d_shift_a, d_scale_a, d_gate_a, d_shift_m, d_scale_m, d_gate_m], axis=1
    )
    d_modul = lax.psum(d_modul_part.astype(jnp.bfloat16), "shard")
    index = lax.axis_index("shard")
    ada_rows = w_ada.shape[0]
    ada_length = b_ada.shape[0]
    own_cond = lax.dynamic_slice_in_dim(cond_act, index * ada_rows, ada_rows, 1)
    grad_w_ada = lax.dot_general(
        own_cond, d_modul, (((0,), (0,)), ((), ())), preferred_element_type=jnp.float32
    )
    grad_b_ada = lax.dynamic_slice_in_dim(
        jnp.sum(d_modul, axis=0, dtype=jnp.float32), index * ada_length, ada_length, 0
    )
    pair_ada = (grad_w_ada, grad_b_ada)
    d_cond_act = backward_product(d_modul, full_ada)
    _, silu_back = jax.vjp(jax.nn.silu, cond_float)
    grad_conditions = silu_back(d_cond_act)[0]
    summed = (
        lax.psum(pair_ada[0].astype(jnp.bfloat16), "replica").astype(jnp.float32),
        lax.psum(pair_ada[1].astype(jnp.bfloat16), "replica").astype(jnp.float32),
        lax.psum(pair_qkv[0].astype(jnp.bfloat16), "replica").astype(jnp.float32),
        lax.psum(pair_qkv[1].astype(jnp.bfloat16), "replica").astype(jnp.float32),
        lax.psum(pair_proj[0].astype(jnp.bfloat16), "replica").astype(jnp.float32),
        lax.psum(pair_proj[1].astype(jnp.bfloat16), "replica").astype(jnp.float32),
        lax.psum(pair_fc1[0].astype(jnp.bfloat16), "replica").astype(jnp.float32),
        lax.psum(pair_fc1[1].astype(jnp.bfloat16), "replica").astype(jnp.float32),
        lax.psum(pair_fc2[0].astype(jnp.bfloat16), "replica").astype(jnp.float32),
        lax.psum(pair_fc2[1].astype(jnp.bfloat16), "replica").astype(jnp.float32),
    )
    pair_ada = (summed[0], summed[1])
    pair_qkv = (summed[2], summed[3])
    pair_proj = (summed[4], summed[5])
    pair_fc1 = (summed[6], summed[7])
    pair_fc2 = (summed[8], summed[9])
    return (
        output,
        grad_latents,
        grad_conditions,
        pair_ada[0],
        pair_ada[1],
        pair_qkv[0],
        pair_qkv[1],
        pair_proj[0],
        pair_proj[1],
        pair_fc1[0],
        pair_fc1[1],
        pair_fc2[0],
        pair_fc2[1],
    )


def solution(mesh):
    placed = (
        P("replica", "shard", None),
        P("replica", None),
        P("replica", "shard", None),
        P("replica"),
        P("shard", None),
        P("shard"),
        P("shard", None),
        P("shard"),
        P("shard", None),
        P("shard"),
        P("shard", None),
        P("shard"),
        P("shard", None),
        P("shard"),
    )
    return jax.shard_map(
        shards,
        mesh=mesh,
        in_specs=placed,
        out_specs=(
            P("replica", "shard", None),
            P("replica", "shard", None),
            P("replica", None),
            P("shard", None),
            P("shard"),
            P("shard", None),
            P("shard"),
            P("shard", None),
            P("shard"),
            P("shard", None),
            P("shard"),
            P("shard", None),
            P("shard"),
        ),
        check_vma=False,
    )
```

profile of v0, /device:TPU:0, one launch (start us, length us, event | category | flops | bytes accessed | tf_op | source)
XLA Modules:
  0.0 1932.2 jit_solution(709824558595214177)
XLA Ops:
  8.8 5.3 all-gather
  15.4 186.2 %all-gather.11.cloned.1.call-done = bf16[1152,6912]{1,0:T(8,128)(2,1)} async-done(((bf16[576,6912]{1,0:T(8,128)(2,1)}), bf16[1152,6912]{1,0:T(8,128)(2,1)}) %all-gather.11.cloned.1.call-update) | async-done | bytes 15925264 | tf_op jit(solution)/shard_map/all_gather | solution.py:79
  201.6 7.7 convolution_add_fusion
  209.4 2.4 fusion.19
  211.7 90.6 %all-gather.13.cloned.1.call-done = bf16[1152,3456]{1,0:T(8,128)(2,1)} async-done(((bf16[576,3456]{1,0:T(8,128)(2,1)}), bf16[1152,3456]{1,0:T(8,128)(2,1)}) %all-gather.13.cloned.1.call-update) | async-done | bytes 7962640 | tf_op jit(solution)/shard_map/all_gather | solution.py:81
  302.4 13.0 fusion.59
  315.4 5.3 copy-done.8
  322.4 4.3 all-gather.1
  326.8 7.8 fusion.26
  339.2 5.1 all-reduce.9
  344.9 4.8 all-gather.2
  349.8 9.6 reshape.214
  359.4 7.1 copy.64
  366.5 4.6 fusion.51
  371.2 14.4 all-gather.17.cloned.1.call-done
  385.5 6.6 copy.63
  392.2 27.5 %multiply_reduce_fusion.1 = (f32[2,16,512]{2,1,0:T(8,128)S(1)}, f32[2,16,512,1024]{3,2,1,0:T(8,128)}) fusion(bf16[2,512,16,72]{1,3,2,0:T(8,128)(2,1)} %copy.64, bf16[2,1024,16,72]{1,3,2,0:T(8,128)(2,1)} %bitcast.98), kind=kOutput, calls=%fused_computation.4 | convolution fusion | flops 2449457152 | bytes 74252288 | tf_op jit(solution)/shard_map/sqhd,skhd->shqk/dot_general | solution.py:125
  419.6 21.3 %exponential_reduce_fusion = f32[2,16,512]{2,1,0:T(8,128)S(1)} fusion(f32[2,16,512,1024]{3,2,1,0:T(8,128)} %get-tuple-element.64, f32[2,16,512]{2,1,0:T(8,128)S(1)} %get-tuple-element.63), kind=kLoop, calls=%fused_computation.3 | loop fusion | flops 50315264 | bytes 67239936 | tf_op jit(solution)/shard_map/reduce_sum | solution.py:128
  440.9 9.3 all-gather.15.cloned.1.call-done
  450.2 6.6 copy.61
  456.9 27.9 %convert_bitcast_fusion = bf16[2,512,16,72]{1,3,2,0:T(8,128)(2,1)} fusion(bf16[2,1024,16,72]{1,3,2,0:T(8,128)(2,1)} %bitcast.94, f32[2,16,512,1024]{3,2,1,0:T(8,128)} %get-tuple-element.64, f32[2,16,512]{2,1,0:T(8,128)S(1)} %log_add_fusion), kind=kOutput, calls=%fused_computation.74 | convolution fusion | flops 2467430400 | bytes 74252288 | tf_op jit(solution)/shard_map/shqk,skhd->sqhd/dot_general | solution.py:130
  484.8 4.1 copy.65
  491.0 6.1 convolution_add_fusion.2
  503.3 120.2 %all-gather.21.cloned.1.call-done = bf16[1152,4608]{1,0:T(8,128)(2,1)} async-done(((bf16[576,4608]{1,0:T(8,128)(2,1)}), bf16[1152,4608]{1,0:T(8,128)(2,1)}) %all-gather.21.cloned.1.call-update) | async-done | bytes 10616848 | tf_op jit(solution)/shard_map/all_gather | solution.py:85
  623.4 19.1 fusion.60
  642.5 113.4 %all-gather.23.cloned.1.call-done = bf16[4608,1152]{1,0:T(8,128)(2,1)} async-done(((bf16[2304,1152]{1,0:T(8,128)(2,1)}), bf16[4608,1152]{1,0:T(8,128)(2,1)}) %all-gather.23.cloned.1.call-update) | async-done | bytes 10616848 | tf_op jit(solution)/shard_map/all_gather | solution.py:87
  756.0 30.4 %fusion.52 = (bf16[4608]{0:T(1024)(128)(2,1)}, bf16[1024,4608]{1,0:T(8,128)(2,1)}) fusion(f32[1024,4608]{1,0:T(8,128)} %fusion.60, f32[4608]{0:T(1024)S(1)} %reshape.203, bf16[1024,1152]{1,0:T(8,128)(2,1)} %bitcast.118, bf16[4608,1152]{1,0:T(8,128)(2,1)} %all-gather.23.cloned.1.call-done), kind=kOutput, calls=%fused_computation.117 | convolution fusion | flops 10975440896 | bytes 41315328 | tf_op jit(solution)/shard_map/dot_general | solution.py:26
  786.3 19.9 %fusion.29 = (f32[1024]{0:T(1024)S(1)}, f32[1024,1152]{1,0:T(8,128)}) fusion(f32[2,1152]{1,0:T(2,128)S(1)} %get-tuple-element.54, bf16[1024,4608]{1,0:T(8,128)(2,1)} %get-tuple-element.41, bf16[1152,4608]{1,0:T(8,128)(2,1)} %all-gather.21.cloned.1.call-done), kind=kOutput, calls=%fused_computation.53 | convolution fusion | flops 10873994240 | bytes 24785920 | tf_op jit(solution)/shard_map/dot_general | solution.py:26
  806.3 20.9 %convolution_add_fusion.1 = f32[1024,1152]{1,0:T(8,128)S(1)} fusion(bf16[4608,1152]{1,0:T(8,128)(2,1)} %all-gather.23.cloned.1.call-done, f32[1152]{0:T(1024)S(1)} %copy-done.40, f32[1024,4608]{1,0:T(8,128)} %fusion.60, f32[4608]{0:T(1024)S(1)} %reshape.203), kind=kOutput, calls=%fused_computation.35 | convolution fusion | flops 10920001536 | bytes 34232832 | tf_op jit(solution)/shard_map/dot_general | solution.py:33
  827.4 4.9 fusion.30
  832.3 4.4 fusion.54
  838.2 3.8 convolution_convert_fusion.5
  841.9 8.5 reshape.215
  850.4 5.8 copy.67
  856.2 26.0 %fusion.32 = bf16[2,16,72,1024]{3,2,1,0:T(8,128)(2,1)} fusion(bf16[2,512,16,72]{1,3,2,0:T(8,128)(2,1)S(1)} %copy.67, f32[2,16,512,1024]{3,2,1,0:T(8,128)} %get-tuple-element.64, f32[2,16,512]{2,1,0:T(8,128)S(1)} %copy-done.10), kind=kOutput, calls=%fused_computation.72 | convolution fusion | flops 2468610048 | bytes 74252288 | tf_op jit(solution)/shard_map/shqk,sqhd->skhd/dot_general | solution.py:192
  882.2 6.7 copy.72
  889.0 49.1 %multiply_reduce_fusion = (f32[2,16,512]{2,1,0:T(8,128)S(1)}, f32[2,16,512,1024]{3,2,1,0:T(8,128)}) fusion(f32[2,16,512,1024]{3,2,1,0:T(8,128)} %get-tuple-element.64, f32[2,16,512]{2,1,0:T(8,128)S(1)} %copy-done.10, bf16[2,512,16,72]{1,3,2,0:T(8,128)(2,1)S(1)} %copy.67, bf16[2,1024,16,72]{1,3,2,0:T(8,128)(2,1)} %bitcast.95), kind=kOutput, calls=%fused_computation.1 | convolution fusion | flops 2483011584 | bytes 141426688 | tf_op jit(solution)/shard_map/sqhd,skhd->shqk/dot_general | solution.py:173
  938.2 53.3 %multiply_convert_fusion = bf16[2,16,512,1024]{3,2,1,0:T(8,128)(2,1)} fusion(f32[2,16,512,1024]{3,2,1,0:T(8,128)} %get-tuple-element.68, f32[2,16,512,1024]{3,2,1,0:T(8,128)} %get-tuple-element.64, f32[2,16,512]{2,1,0:T(8,128)S(1)} %get-tuple-element.67, f32[2,16,512]{2,1,0:T(8,128)S(1)} %copy-done.10), kind=kLoop, calls=%fused_computation | loop fusion | flops 83886080 | bytes 167903232 | tf_op jit(solution)/shard_map/convert_element_type | solution.py:177
  991.5 18.7 multiply_convert_fusion.2
  1010.2 6.7 copy.70
  1018.6 6.4 convolution_convert_fusion.4
  1025.0 23.4 %convolution_convert_fusion = bf16[4608,1152]{1,0:T(8,128)(2,1)} fusion(bf16[1024,1152]{1,0:T(8,128)(2,1)} %bitcast.119, f32[1024,4608]{1,0:T(8,128)} %fusion.60, f32[4608]{0:T(1024)S(1)} %copy-done.33), kind=kOutput, calls=%fused_computation.8 | convolution fusion | flops 10924130304 | bytes 31868928 | tf_op jit(solution)/shard_map/dot_general | solution.py:45
  1050.1 17.4 convolution_convert_fusion.1
  1067.7 18.1 fusion.58
  1085.7 2.4 copy.68
  1090.2 4.4 copy.74
  1094.6 4.3 copy.73
  1098.9 13.4 convolution_convert_fusion.2
  1113.1 16.0 fusion.28
  1131.2 5.2 fusion.24
  1136.6 6.6 multiply_reduce_fusion.3
  1143.2 9.1 all-reduce.8
  1152.4 10.5 fusion.41
  1162.9 5.7 convolution_convert_fusion.3
  1168.5 76.7 %reduce-scatter.17.cloned.1.call-done = bf16[2304,1152]{1,0:T(8,128)(2,1)} async-done(((bf16[4608,1152]{1,0:T(8,128)(2,1)}), bf16[2304,1152]{1,0:T(8,128)(2,1)}) %reduce-scatter.17.cloned.1.call-update) | async-done | bytes 5308432 | tf_op jit(solution)/shard_map/reduce_scatter | solution.py:44
  1245.2 126.1 %reduce-scatter.15.cloned.1.call-done = bf16[576,4608]{1,0:T(8,128)(2,1)} async-done(((bf16[1152,4608]{1,0:T(8,128)(2,1)}), bf16[576,4608]{1,0:T(8,128)(2,1)}) %reduce-scatter.15.cloned.1.call-update) | async-done | bytes 5308432 | tf_op jit(solution)/shard_map/reduce_scatter | solution.py:44
  1371.4 97.6 %reduce-scatter.11.cloned.1.call-done = bf16[576,3456]{1,0:T(8,128)(2,1)} async-done(((bf16[1152,3456]{1,0:T(8,128)(2,1)}), bf16[576,3456]{1,0:T(8,128)(2,1)}) %reduce-scatter.11.cloned.1.call-update) | async-done | bytes 3981328 | tf_op jit(solution)/shard_map/reduce_scatter | solution.py:44
  1471.5 64.6 %all-reduce.6 = (bf16[3456]{0:T(1024)(128)(2,1)S(1)}, bf16[1152]{0:T(1024)(128)(2,1)S(1)}, bf16[576]{0:T(1024)(128)(2,1)S(1)}, bf16[2304]{0:T(1024)(128)(2,1)S(1)}, bf16[576]{0:T(1024)(128)(2,1)S(1)}) all-reduce(bf16[3456]{0:T(1024)(128)(2,1)S(1)} %dynamic_slice.11, ...), channel_id=1, replica_groups=mesh['replica'=16,'shard'=2] {'replica'}, use_global_device_ids=true, to_apply=%region_22.23 | all-reduce | flops 8064 | bytes 32256 | tf_op jit(solution)/shard_map/psum | solution.py:237
  1539.1 356.0 %all-reduce.12.cloned.1.call-done = (bf16[576,6912]{1,0:T(8,128)(2,1)}, bf16[576,3456]{1,0:T(8,128)(2,1)}, bf16[576,1152]{1,0:T(8,128)(2,1)}, bf16[576,4608]{1,0:T(8,128)(2,1)}, bf16[2304,1152]{1,0:T(8,128)(2,1)}) async-done(((bf16[576,6912]{1,0:T(8,128)(2,1)}, bf16[576,3456]{1,0:T(8,128)(2,1)}, bf16[576,1152]{1,0:T(8,128)(2,1)}, bf16[576,4608]{1,0:T(8,128)(2,1)}, bf16[2304,1152]{1,0:T(8,128)(2,1)}), ...) | async-done | bytes 23887888 | tf_op jit(solution)/shard_map/psum | solution.py:236
  1895.1 3.2 convert_element_type.232
  1898.3 10.4 convert_element_type.222
  1908.7 6.1 convert_element_type.227
  1914.8 5.6 convert_element_type.235
  1920.4 4.8 convert_element_type.238
  (203 shorter events, 30.1 us)
Async XLA Ops:
  7.2 7.0 copy-start.1
  7.2 194.4 %all-gather.11.cloned.1.call-start = ((), (), s32[]{:S(2)}) async-start(), calls=%async_computation.6 | async-start | bytes 23887872 | tf_op jit(solution)/shard_map/all_gather | solution.py:79
  7.9 193.7 %copy-start.30 = (bf16[2,1152]{1,0:T(2,128)(2,1)S(1)}, bf16[2,1152]{1,0:T(2,128)(2,1)}, u32[]{:S(2)}) copy-start(bf16[2,1152]{1,0:T(2,128)(2,1)} %param.15) | copy-start | bytes 13828
  7.9 294.4 %all-gather.13.cloned.1.call-start = ((), (), s32[]{:S(2)}) async-start(), calls=%async_computation.7 | async-start | bytes 11943936 | tf_op jit(solution)/shard_map/all_gather | solution.py:81
  8.7 376.9 %all-gather.17.cloned.1.call-start = ((), (), s32[]{:S(2)}) async-start(), calls=%async_computation.9 | async-start | bytes 7077888 | tf_op jit(solution)/shard_map/all_gather | solution.py:118
  14.6 194.7 %copy-start.20 = (f32[2,512]{1,0:T(2,128)}, f32[2,512]{1,0:T(2,128)S(1)}, u32[]{:S(2)}) copy-start(f32[2,512]{1,0:T(2,128)S(1)} %broadcast_multiply_fusion.5) | copy-start | bytes 12292
  15.4 193.9 %copy-start.28 = (f32[2,512]{1,0:T(2,128)}, f32[2,512]{1,0:T(2,128)S(1)}, u32[]{:S(2)}) copy-start(f32[2,512]{1,0:T(2,128)S(1)} %add_rsqrt_fusion.1) | copy-start | bytes 12292
  209.3 106.1 %copy-start.16 = (f32[2,1152]{1,0:T(2,128)}, f32[2,1152]{1,0:T(2,128)S(1)}, u32[]{:S(2)}) copy-start(f32[2,1152]{1,0:T(2,128)S(1)} %get-tuple-element.56) | copy-start | bytes 27652
  209.3 157.2 %copy-start.24 = (f32[2,1152]{1,0:T(2,128)}, f32[2,1152]{1,0:T(2,128)S(1)}, u32[]{:S(2)}) copy-start(f32[2,1152]{1,0:T(2,128)S(1)} %get-tuple-element.52) | copy-start | bytes 27652
  209.3 287.8 %copy-start.22 = (f32[2,1152]{1,0:T(2,128)}, f32[2,1152]{1,0:T(2,128)S(1)}, u32[]{:S(2)}) copy-start(f32[2,1152]{1,0:T(2,128)S(1)} %get-tuple-element.57) | copy-start | bytes 27652
  315.4 5.3 copy-start.8
  322.4 127.8 %all-gather.15.cloned.1.call-start = ((), (), s32[]{:S(2)}) async-start(), calls=%async_computation.8 | async-start | bytes 7077888 | tf_op jit(solution)/shard_map/all_gather | solution.py:119
  334.7 156.4 %all-gather.19.cloned.1.call-start = ((), (), s32[]{:S(2)}) async-start(), calls=%async_computation.10 | async-start | bytes 3981312 | tf_op jit(solution)/shard_map/all_gather | solution.py:83
  335.2 2.1 copy-start.46
  335.3 3.5 copy-start.47
  335.3 3.7 copy-start.48
  335.3 9.7 copy-start.42
  335.3 288.1 %all-gather.21.cloned.1.call-start = ((), (), s32[]{:S(2)}) async-start(), calls=%async_computation.11 | async-start | bytes 15925248 | tf_op jit(solution)/shard_map/all_gather | solution.py:85
  335.9 420.1 %all-gather.23.cloned.1.call-start = ((), (), s32[]{:S(2)}) async-start(), calls=%async_computation.12 | async-start | bytes 15925248 | tf_op jit(solution)/shard_map/all_gather | solution.py:87
  336.6 753.6 %reduce-scatter.9.cloned.1.call-start = ((), (), s32[]{:S(2)}) async-start(), calls=%async_computation.14 | async-start | bytes 7077888 | tf_op jit(solution)/shard_map/reduce_scatter | solution.py:202
  337.3 29.2 %copy-start.43 = (f32[2]{0:T(128)}, f32[2]{0:T(128)S(1)}, u32[]{:S(2)}) copy-start(f32[2]{0:T(128)S(1)} %compare_convert_fusion) | copy-start | bytes 28
  349.8 456.5 %copy-start.32 = (f32[4608]{0:T(1024)}, f32[4608]{0:T(1024)S(1)}, u32[]{:S(2)}) copy-start(f32[4608]{0:T(1024)S(1)} %reshape.203) | copy-start | bytes 55300
  456.8 27.9 %copy-start.9 = (f32[2,16,512]{2,1,0:T(8,128)}, f32[2,16,512]{2,1,0:T(8,128)S(1)}, u32[]{:S(2)}) copy-start(f32[2,16,512]{2,1,0:T(8,128)S(1)} %log_add_fusion) | copy-start | bytes 196612
  497.2 2.5 copy-start.7
  499.6 2.8 copy-start
  499.6 3.6 copy-start.18
  500.2 142.3 %copy-start.26 = (f32[2,512]{1,0:T(2,128)}, f32[2,512]{1,0:T(2,128)S(1)}, u32[]{:S(2)}) copy-start(f32[2,512]{1,0:T(2,128)S(1)} %add_rsqrt_fusion) | copy-start | bytes 12292
  503.3 139.3 %copy-start.13 = (bf16[2,512,1152]{2,1,0:T(8,128)(2,1)}, bf16[2,512,1152]{2,1,0:T(8,128)(2,1)S(1)}, u32[]{:S(2)}) copy-start(bf16[2,512,1152]{2,1,0:T(8,128)(2,1)S(1)} %add_convert_fusion) | copy-start | bytes 7077892
  786.3 19.9 %copy-start.40 = (f32[1152]{0:T(1024)S(1)}, f32[1152]{0:T(1024)}, u32[]{:S(2)}) copy-start(f32[1152]{0:T(1024)} %convert_element_type.204) | copy-start | bytes 13828
  786.3 41.0 %slice-start = ((s8[4718592]{0:T(1024)(128)(4,1)}), s8[524288]{0:T(1024)(128)(4,1)S(1)}, s32[]{:S(2)}) async-start(s8[4718592]{0:T(1024)(128)(4,1)} %bitcast.92), calls=%async_computation.20 | async-start | bytes 1048576
  806.3 21.0 %slice-start.1 = ((s8[4718592]{0:T(1024)(128)(4,1)}), s8[4194304]{0:T(1024)(128)(4,1)S(1)}, s32[]{:S(2)}) async-start(s8[4718592]{0:T(1024)(128)(4,1)} %bitcast.92), calls=%async_computation.21 | async-start | bytes 8388608
  806.3 21.0 %copy-start.4 = (f32[1024,1152]{1,0:T(8,128)S(1)}, f32[1024,1152]{1,0:T(8,128)}, u32[]{:S(2)}) copy-start(f32[1024,1152]{1,0:T(8,128)} %get-tuple-element.66) | copy-start | bytes 14155780
  806.3 21.0 %copy-start.6 = (bf16[2,512,1152]{2,1,0:T(8,128)(2,1)S(1)}, bf16[2,512,1152]{2,1,0:T(8,128)(2,1)}, u32[]{:S(2)}) copy-start(bf16[2,512,1152]{2,1,0:T(8,128)(2,1)} %param.16) | copy-start | bytes 7077892
  806.3 21.0 %copy-start.19 = (f32[2,512]{1,0:T(2,128)S(1)}, f32[2,512]{1,0:T(2,128)}, u32[]{:S(2)}) copy-start(f32[2,512]{1,0:T(2,128)} %copy-done.18) | copy-start | bytes 12292
  806.3 21.0 %copy-start.25 = (f32[2,1152]{1,0:T(2,128)S(1)}, f32[2,1152]{1,0:T(2,128)}, u32[]{:S(2)}) copy-start(f32[2,1152]{1,0:T(2,128)} %copy-done.24) | copy-start | bytes 27652
  806.3 21.0 %copy-start.27 = (f32[2,512]{1,0:T(2,128)S(1)}, f32[2,512]{1,0:T(2,128)}, u32[]{:S(2)}) copy-start(f32[2,512]{1,0:T(2,128)} %copy-done.26) | copy-start | bytes 12292
  806.3 21.0 %copy-start.44 = (f32[2]{0:T(128)S(1)}, f32[2]{0:T(128)}, u32[]{:S(2)}) copy-start(f32[2]{0:T(128)} %copy-done.43) | copy-start | bytes 28
  827.4 4.9 copy-start.23
  832.3 5.9 copy-start.49
  850.4 5.8 copy-start.10
  889.0 205.6 %reduce-scatter.7.cloned.1.call-start = ((), (), s32[]{:S(2)}) async-start(), calls=%async_computation.13 | async-start | bytes 7077888 | tf_op jit(solution)/shard_map/reduce_scatter | solution.py:199
  938.2 53.3 %copy-start.5 = (bf16[2,512,16,72]{1,3,2,0:T(8,128)(2,1)S(1)}, bf16[2,512,16,72]{1,3,2,0:T(8,128)(2,1)}, u32[]{:S(2)}) copy-start(bf16[2,512,16,72]{1,3,2,0:T(8,128)(2,1)} %copy.64) | copy-start | bytes 7077892
  1016.9 8.1 copy-start.33
  1016.9 151.6 %reduce-scatter.13.cloned.1.call-start = ((), (), s32[]{:S(2)}) async-start(), calls=%async_computation.16 | async-start | bytes 3981312 | tf_op jit(solution)/shard_map/reduce_scatter | solution.py:44
  1025.0 220.2 %reduce-scatter.17.cloned.1.call-start = ((), (), s32[]{:S(2)}) async-start(), calls=%async_computation.18 | async-start | bytes 15925248 | tf_op jit(solution)/shard_map/reduce_scatter | solution.py:44
  1048.5 322.9 %reduce-scatter.15.cloned.1.call-start = ((), (), s32[]{:S(2)}) async-start(), calls=%async_computation.17 | async-start | bytes 15925248 | tf_op jit(solution)/shard_map/reduce_scatter | solution.py:44
  1067.6 401.3 %reduce-scatter.11.cloned.1.call-start = ((), (), s32[]{:S(2)}) async-start(), calls=%async_computation.15 | async-start | bytes 11943936 | tf_op jit(solution)/shard_map/reduce_scatter | solution.py:44
  1090.2 8.7 copy-start.15
  1112.4 782.8 %all-reduce.12.cloned.1.call-start = ((), (), s32[]{:S(2)}) async-start(), calls=%async_computation.19 | async-start | bytes 47775744 | tf_op jit(solution)/shard_map/psum | solution.py:236
  1113.0 18.1 copy-start.2
  1113.0 18.1 copy-start.21
  1113.0 18.1 copy-start.29
  1131.2 5.3 copy-start.3
  1136.5 6.7 copy-start.36
  1136.5 6.7 copy-start.35
  1136.5 6.7 copy-start.34
  1136.5 6.7 copy-start.37
  1136.5 6.7 copy-start.38
  1136.5 6.7 copy-start.39
  1136.6 15.8 copy-start.31
  1895.1 19.7 %slice-start.4 = ((s8[5308416]{0:T(1024)(128)(4,1)}), s8[4194304]{0:T(1024)(128)(4,1)S(1)}, s32[]{:S(2)}) async-start(s8[5308416]{0:T(1024)(128)(4,1)} %bitcast.110), calls=%async_computation.24 | async-start | bytes 8388608
  1898.3 16.5 slice-start.5
  1908.7 11.7 slice-start.2
  1914.8 5.6 slice-start.3
  (6 other events, 8.7 us)
Sparse Core Ops, SparseCore 0:
  9.6 191.9 all-gather.10
  203.1 99.1 all-gather.12
  322.5 63.0 all-gather.16
  387.5 62.6 all-gather.14
  451.6 39.3 all-gather.18
  492.4 130.9 all-gather.20
  625.0 130.9 all-gather.22
  889.1 59.9 reduce-scatter.8
  1017.0 60.0 reduce-scatter.6
  1079.8 37.9 reduce-scatter.12
  1120.7 124.4 reduce-scatter.16
  1248.1 123.2 reduce-scatter.14
  1374.2 94.6 reduce-scatter.10
  1475.5 419.5 all-reduce.11
where the time goes:
time: 1940 us; the launch traced here: 1930 us
  waiting for transfers between devices  1190 us (61%)
  matrix products  381 us (20%)
  other arithmetic  150 us (8%)
  local copies, waits for them, and re-layouts  94.9 us (5%)
  blocking collectives  93.2 us (5%)
    psum x1, waiting for transfers between devices, shards(): lax.psum(pair_ada[0].astype(jnp.bfloat16), 'replica').astype(jnp.float32)  356 us
    reduce_scatter x4, waiting for transfers between devices, owner_grads(): lax.psum_scatter(lax.dot_general(columns, grads, (((0,), (0,)), ((), ()))...  300 us
    all_gather x1, waiting for transfers between devices, shards(): lax.all_gather(w_ada, 'shard', axis=0, tiled=True)  186 us
    all_gather x1, waiting for transfers between devices, shards(): lax.all_gather(w_fc1, 'shard', axis=0, tiled=True)  120 us
    all_gather x1, waiting for transfers between devices, shards(): lax.all_gather(w_fc2, 'shard', axis=0, tiled=True)  113 us
    all_gather x1, waiting for transfers between devices, shards(): lax.all_gather(w_qkv, 'shard', axis=0, tiled=True)  90.6 us
    dot_general x5, matrix products, contract_last(): lax.dot_general(left, right, (((1,), (1,)), ((), ())), preferred_element_...  80.5 us
    dot_general x5, matrix products, forward_product(): jnp.dot(inputs, whole_pair[0], preferred_element_type=jnp.float32)  66.9 us
  transfers between devices with their start and end apart: 14, of which 11 were waited for; matrix products, arithmetic and copies ran while one was open for 23% of the time, Pallas kernels for 0%

commit v1 on v0

--- a/solution.py
+++ b/solution.py
@@ -233,7 +233,9 @@
     _, silu_back = jax.vjp(jax.nn.silu, cond_float)
     grad_conditions = silu_back(d_cond_act)[0]
     summed = (
-        lax.psum(pair_ada[0].astype(jnp.bfloat16), "replica").astype(jnp.float32),
+        jnp.sum(lax.all_gather(pair_ada[0].astype(jnp.bfloat16), "replica"), axis=0).astype(
+            jnp.float32
+        ),
         lax.psum(pair_ada[1].astype(jnp.bfloat16), "replica").astype(jnp.float32),
         lax.psum(pair_qkv[0].astype(jnp.bfloat16), "replica").astype(jnp.float32),
         lax.psum(pair_qkv[1].astype(jnp.bfloat16), "replica").astype(jnp.float32),

time: 1940 us -> 2440 us (1.26)
  waiting for transfers between devices: 1190 us -> 1650 us
  other arithmetic: 150 us -> 195 us
    all_gather x0 -> x1, waiting for transfers between devices: none -> 591 us  [shards(): lax.all_gather(pair_ada[0].astype(jnp.bfloat16), 'replica')]
    psum x1, waiting for transfers between devices: 356 us -> 168 us  [shards(): lax.psum(pair_qkv[0].astype(jnp.bfloat16), 'replica').astype(jnp.float32)]
    reduce_scatter x4, waiting for transfers between devices: 300 us -> 355 us  [owner_grads(): lax.psum_scatter(lax.dot_general(columns, grads, (((0,), (0,)), ((), ()))...]
    reduce_sum x0 -> x1, other arithmetic: none -> 43.4 us  [shards(): jnp.sum(lax.all_gather(pair_ada[0].astype(jnp.bfloat16), 'replica'), axis=0)]
  transfers between devices with their start and end apart: 14 -> 15, of which waited for: 11 -> 13; matrix products, arithmetic and copies ran while one was open for 23% -> 19% of each run, Pallas kernels for 0% -> 0%
where the time goes in v1:
time: 2440 us; the launch traced here: 2430 us
  waiting for transfers between devices  1650 us (68%)
  matrix products  381 us (16%)
  other arithmetic  195 us (8%)
  local copies, waits for them, and re-layouts  94.8 us (4%)
  blocking collectives  91 us (4%)
    all_gather x1, waiting for transfers between devices, shards(): lax.all_gather(pair_ada[0].astype(jnp.bfloat16), 'replica')  591 us
    reduce_scatter x4, waiting for transfers between devices, owner_grads(): lax.psum_scatter(lax.dot_general(columns, grads, (((0,), (0,)), ((), ()))...  355 us
    all_gather x1, waiting for transfers between devices, shards(): lax.all_gather(w_ada, 'shard', axis=0, tiled=True)  186 us
    psum x1, waiting for transfers between devices, shards(): lax.psum(pair_qkv[0].astype(jnp.bfloat16), 'replica').astype(jnp.float32)  168 us
    all_gather x1, waiting for transfers between devices, shards(): lax.all_gather(w_fc1, 'shard', axis=0, tiled=True)  120 us
    all_gather x1, waiting for transfers between devices, shards(): lax.all_gather(w_fc2, 'shard', axis=0, tiled=True)  113 us
    all_gather x1, waiting for transfers between devices, shards(): lax.all_gather(w_qkv, 'shard', axis=0, tiled=True)  90.6 us
    dot_general x5, matrix products, contract_last(): lax.dot_general(left, right, (((1,), (1,)), ((), ())), preferred_element_...  80.8 us
  transfers between devices with their start and end apart: 15, of which 13 were waited for; matrix products, arithmetic and copies ran while one was open for 19% of the time, Pallas kernels for 0%

profile of v1, /device:TPU:0, one launch (start us, length us, event | category | flops | bytes accessed | tf_op | source)
XLA Modules:
  0.0 2432.9 jit_solution(6386350697523545702)
XLA Ops:
  8.8 5.3 all-gather.1
  15.4 186.2 %all-gather.13.cloned.1.call-done = bf16[1152,6912]{1,0:T(8,128)(2,1)} async-done(((bf16[576,6912]{1,0:T(8,128)(2,1)}), bf16[1152,6912]{1,0:T(8,128)(2,1)}) %all-gather.13.cloned.1.call-update) | async-done | bytes 15925264 | tf_op jit(solution)/shard_map/all_gather | solution.py:79
  201.6 7.7 convolution_add_fusion
  211.8 90.6 %all-gather.15.cloned.1.call-done = bf16[1152,3456]{1,0:T(8,128)(2,1)} async-done(((bf16[576,3456]{1,0:T(8,128)(2,1)}), bf16[1152,3456]{1,0:T(8,128)(2,1)}) %all-gather.15.cloned.1.call-update) | async-done | bytes 7962640 | tf_op jit(solution)/shard_map/all_gather | solution.py:81
  302.4 13.0 fusion.59
  315.4 5.3 copy-done.8
  322.4 4.3 all-gather.2
  326.8 7.8 fusion.26
  339.1 5.1 all-reduce.9
  344.9 4.8 all-gather.3
  349.7 9.6 reshape.215
  359.3 7.2 copy.64
  366.5 4.6 fusion.51
  371.1 14.4 all-gather.19.cloned.1.call-done
  385.5 6.6 copy.63
  392.2 27.5 %multiply_reduce_fusion.1 = (f32[2,16,512]{2,1,0:T(8,128)S(1)}, f32[2,16,512,1024]{3,2,1,0:T(8,128)}) fusion(bf16[2,512,16,72]{1,3,2,0:T(8,128)(2,1)} %copy.64, bf16[2,1024,16,72]{1,3,2,0:T(8,128)(2,1)} %bitcast.99), kind=kOutput, calls=%fused_computation.4 | convolution fusion | flops 2449457152 | bytes 74252288 | tf_op jit(solution)/shard_map/sqhd,skhd->shqk/dot_general | solution.py:125
  419.6 21.3 exponential_reduce_fusion
  440.9 9.3 all-gather.17.cloned.1.call-done
  450.2 6.6 copy.61
  456.9 27.9 %convert_bitcast_fusion = bf16[2,512,16,72]{1,3,2,0:T(8,128)(2,1)} fusion(bf16[2,1024,16,72]{1,3,2,0:T(8,128)(2,1)} %bitcast.95, f32[2,16,512,1024]{3,2,1,0:T(8,128)} %get-tuple-element.63, f32[2,16,512]{2,1,0:T(8,128)S(1)} %log_add_fusion), kind=kOutput, calls=%fused_computation.74 | convolution fusion | flops 2467430400 | bytes 74252288 | tf_op jit(solution)/shard_map/shqk,skhd->sqhd/dot_general | solution.py:130
  484.8 4.1 copy.65
  491.0 6.1 convolution_add_fusion.2
  503.3 120.2 %all-gather.23.cloned.1.call-done = bf16[1152,4608]{1,0:T(8,128)(2,1)} async-done(((bf16[576,4608]{1,0:T(8,128)(2,1)}), bf16[1152,4608]{1,0:T(8,128)(2,1)}) %all-gather.23.cloned.1.call-update) | async-done | bytes 10616848 | tf_op jit(solution)/shard_map/all_gather | solution.py:85
  623.4 19.1 fusion.60
  642.5 113.4 %all-gather.25.cloned.1.call-done = bf16[4608,1152]{1,0:T(8,128)(2,1)} async-done(((bf16[2304,1152]{1,0:T(8,128)(2,1)}), bf16[4608,1152]{1,0:T(8,128)(2,1)}) %all-gather.25.cloned.1.call-update) | async-done | bytes 10616848 | tf_op jit(solution)/shard_map/all_gather | solution.py:87
  756.0 30.6 %fusion.52 = (bf16[4608]{0:T(1024)(128)(2,1)}, bf16[1024,4608]{1,0:T(8,128)(2,1)}) fusion(f32[1024,4608]{1,0:T(8,128)} %fusion.60, f32[4608]{0:T(1024)S(1)} %reshape.204, bf16[1024,1152]{1,0:T(8,128)(2,1)} %bitcast.119, bf16[4608,1152]{1,0:T(8,128)(2,1)} %all-gather.25.cloned.1.call-done), kind=kOutput, calls=%fused_computation.117 | convolution fusion | flops 10975440896 | bytes 41315328 | tf_op jit(solution)/shard_map/dot_general | solution.py:26
  786.6 19.9 fusion.29
  806.6 20.9 convolution_add_fusion.1
  827.6 4.9 fusion.30
  832.5 4.4 fusion.54
  838.4 3.7 convolution_convert_fusion.5
  842.1 8.5 reshape.216
  850.6 5.8 copy.67
  856.5 26.0 %fusion.32 = bf16[2,16,72,1024]{3,2,1,0:T(8,128)(2,1)} fusion(bf16[2,512,16,72]{1,3,2,0:T(8,128)(2,1)S(1)} %copy.67, f32[2,16,512,1024]{3,2,1,0:T(8,128)} %get-tuple-element.63, f32[2,16,512]{2,1,0:T(8,128)S(1)} %copy-done.10), kind=kOutput, calls=%fused_computation.72 | convolution fusion | flops 2468610048 | bytes 74252288 | tf_op jit(solution)/shard_map/shqk,sqhd->skhd/dot_general | solution.py:192
  882.4 6.7 copy.72
  889.2 49.1 %multiply_reduce_fusion = (f32[2,16,512]{2,1,0:T(8,128)S(1)}, f32[2,16,512,1024]{3,2,1,0:T(8,128)}) fusion(f32[2,16,512,1024]{3,2,1,0:T(8,128)} %get-tuple-element.63, f32[2,16,512]{2,1,0:T(8,128)S(1)} %copy-done.10, bf16[2,512,16,72]{1,3,2,0:T(8,128)(2,1)S(1)} %copy.67, bf16[2,1024,16,72]{1,3,2,0:T(8,128)(2,1)} %bitcast.96), kind=kOutput, calls=%fused_computation.1 | convolution fusion | flops 2483011584 | bytes 141426688 | tf_op jit(solution)/shard_map/sqhd,skhd->shqk/dot_general | solution.py:173
  938.4 53.4 %multiply_convert_fusion = bf16[2,16,512,1024]{3,2,1,0:T(8,128)(2,1)} fusion(f32[2,16,512,1024]{3,2,1,0:T(8,128)} %get-tuple-element.67, f32[2,16,512,1024]{3,2,1,0:T(8,128)} %get-tuple-element.63, f32[2,16,512]{2,1,0:T(8,128)S(1)} %get-tuple-element.66, f32[2,16,512]{2,1,0:T(8,128)S(1)} %copy-done.10), kind=kLoop, calls=%fused_computation | loop fusion | flops 83886080 | bytes 167903232 | tf_op jit(solution)/shard_map/convert_element_type | solution.py:177
  991.8 18.7 multiply_convert_fusion.2
  1010.4 6.7 copy.70
  1018.8 6.4 convolution_convert_fusion.4
  1025.3 23.5 convolution_convert_fusion
  1050.4 17.4 convolution_convert_fusion.1
  1068.0 18.1 fusion.58
  1090.5 4.4 copy.74
  1094.9 4.3 copy.73
  1099.2 13.4 convolution_convert_fusion.2
  1112.7 5.3 reduce-scatter.13.cloned.1.call-done
  1118.0 126.2 %reduce-scatter.17.cloned.1.call-done = bf16[2304,1152]{1,0:T(8,128)(2,1)} async-done(((bf16[4608,1152]{1,0:T(8,128)(2,1)}), bf16[2304,1152]{1,0:T(8,128)(2,1)}) %reduce-scatter.17.cloned.1.call-update) | async-done | bytes 5308432 | tf_op jit(solution)/shard_map/reduce_scatter | solution.py:44
  1244.2 126.2 %reduce-scatter.15.cloned.1.call-done = bf16[576,4608]{1,0:T(8,128)(2,1)} async-done(((bf16[1152,4608]{1,0:T(8,128)(2,1)}), bf16[576,4608]{1,0:T(8,128)(2,1)}) %reduce-scatter.15.cloned.1.call-update) | async-done | bytes 5308432 | tf_op jit(solution)/shard_map/reduce_scatter | solution.py:44
  1370.4 97.6 %reduce-scatter.11.cloned.1.call-done = bf16[576,3456]{1,0:T(8,128)(2,1)} async-done(((bf16[1152,3456]{1,0:T(8,128)(2,1)}), bf16[576,3456]{1,0:T(8,128)(2,1)}) %reduce-scatter.11.cloned.1.call-update) | async-done | bytes 3981328 | tf_op jit(solution)/shard_map/reduce_scatter | solution.py:44
  1468.6 16.0 fusion.28
  1486.8 5.2 fusion.24
  1492.1 6.3 multiply_reduce_fusion.3
  1498.6 7.6 all-reduce.8
  1506.3 10.5 fusion.41
  1516.8 5.7 convolution_convert_fusion.3
  1524.8 63.8 %all-reduce.6 = (bf16[3456]{0:T(1024)(128)(2,1)S(1)}, bf16[1152]{0:T(1024)(128)(2,1)S(1)}, bf16[576]{0:T(1024)(128)(2,1)S(1)}, bf16[2304]{0:T(1024)(128)(2,1)S(1)}, bf16[576]{0:T(1024)(128)(2,1)S(1)}) all-reduce(bf16[3456]{0:T(1024)(128)(2,1)S(1)} %dynamic_slice.11, ...), channel_id=1, replica_groups=mesh['replica'=16,'shard'=2] {'replica'}, use_global_device_ids=true, to_apply=%region_22.23 | all-reduce | flops 8064 | bytes 32256 | tf_op jit(solution)/shard_map/psum | solution.py:239
  1591.6 168.3 %all-reduce.12.cloned.1.call-done = (bf16[576,3456]{1,0:T(8,128)(2,1)}, bf16[576,1152]{1,0:T(8,128)(2,1)}, bf16[576,4608]{1,0:T(8,128)(2,1)}, bf16[2304,1152]{1,0:T(8,128)(2,1)}) async-done(((bf16[576,3456]{1,0:T(8,128)(2,1)}, bf16[576,1152]{1,0:T(8,128)(2,1)}, bf16[576,4608]{1,0:T(8,128)(2,1)}, bf16[2304,1152]{1,0:T(8,128)(2,1)}), (bf16[576,3456]{1,0:T(8,128)(2,1)}, bf16[576,1152]{1,0:T(8,128)(2,1)}, ...) | async-done | bytes 15925264 | tf_op jit(solution)/shard_map/psum | solution.py:240
  1763.0 4.6 convert_element_type.229
  1767.7 8.4 convert_element_type.237
  1776.1 4.8 convert_element_type.240
  1781.0 591.2 %all-gather.27.cloned.1.call-done = bf16[9216,6912]{1,0:T(8,128)(2,1)} async-done(((bf16[576,6912]{1,0:T(8,128)(2,1)}), bf16[9216,6912]{1,0:T(8,128)(2,1)}) %all-gather.27.cloned.1.call-update) | async-done | bytes 127402000 | tf_op jit(solution)/shard_map/all_gather | solution.py:236
  2372.2 43.4 %reduce_sum.237 = bf16[576,6912]{1,0:T(8,128)(2,1)} reduce(bf16[16,576,6912]{2,1,0:T(8,128)(2,1)} %bitcast.24, bf16[]{:T(256)} %constant.53.clone.1), dimensions={0}, to_apply=%region_20.21 | reduce | flops 59719680 | bytes 135364608 | tf_op jit(solution)/shard_map/reduce_sum | solution.py:236
  2415.6 10.3 convert_element_type.224
  (209 shorter events, 38.0 us)
Async XLA Ops:
  7.2 7.0 copy-start.1
  7.2 194.4 %all-gather.13.cloned.1.call-start = ((), (), s32[]{:S(2)}) async-start(), calls=%async_computation.6 | async-start | bytes 23887872 | tf_op jit(solution)/shard_map/all_gather | solution.py:79
  7.9 193.7 %copy-start.31 = (bf16[2,1152]{1,0:T(2,128)(2,1)S(1)}, bf16[2,1152]{1,0:T(2,128)(2,1)}, u32[]{:S(2)}) copy-start(bf16[2,1152]{1,0:T(2,128)(2,1)} %param.15) | copy-start | bytes 13828
  7.9 294.4 %all-gather.15.cloned.1.call-start = ((), (), s32[]{:S(2)}) async-start(), calls=%async_computation.7 | async-start | bytes 11943936 | tf_op jit(solution)/shard_map/all_gather | solution.py:81
  8.7 376.9 %all-gather.19.cloned.1.call-start = ((), (), s32[]{:S(2)}) async-start(), calls=%async_computation.9 | async-start | bytes 7077888 | tf_op jit(solution)/shard_map/all_gather | solution.py:118
  14.6 194.7 %copy-start.21 = (f32[2,512]{1,0:T(2,128)}, f32[2,512]{1,0:T(2,128)S(1)}, u32[]{:S(2)}) copy-start(f32[2,512]{1,0:T(2,128)S(1)} %broadcast_multiply_fusion.5) | copy-start | bytes 12292
  15.4 193.9 %copy-start.29 = (f32[2,512]{1,0:T(2,128)}, f32[2,512]{1,0:T(2,128)S(1)}, u32[]{:S(2)}) copy-start(f32[2,512]{1,0:T(2,128)S(1)} %add_rsqrt_fusion.1) | copy-start | bytes 12292
  209.3 106.1 %copy-start.17 = (f32[2,1152]{1,0:T(2,128)}, f32[2,1152]{1,0:T(2,128)S(1)}, u32[]{:S(2)}) copy-start(f32[2,1152]{1,0:T(2,128)S(1)} %get-tuple-element.55) | copy-start | bytes 27652
  209.3 157.2 %copy-start.25 = (f32[2,1152]{1,0:T(2,128)}, f32[2,1152]{1,0:T(2,128)S(1)}, u32[]{:S(2)}) copy-start(f32[2,1152]{1,0:T(2,128)S(1)} %get-tuple-element.51) | copy-start | bytes 27652
  209.3 287.8 %copy-start.23 = (f32[2,1152]{1,0:T(2,128)}, f32[2,1152]{1,0:T(2,128)S(1)}, u32[]{:S(2)}) copy-start(f32[2,1152]{1,0:T(2,128)S(1)} %get-tuple-element.56) | copy-start | bytes 27652
  315.4 5.3 copy-start.8
  322.4 127.8 %all-gather.17.cloned.1.call-start = ((), (), s32[]{:S(2)}) async-start(), calls=%async_computation.8 | async-start | bytes 7077888 | tf_op jit(solution)/shard_map/all_gather | solution.py:119
  334.7 156.4 %all-gather.21.cloned.1.call-start = ((), (), s32[]{:S(2)}) async-start(), calls=%async_computation.10 | async-start | bytes 3981312 | tf_op jit(solution)/shard_map/all_gather | solution.py:83
  335.3 3.4 copy-start.48
  335.3 3.6 copy-start.49
  335.3 9.6 copy-start.43
  335.3 288.1 %all-gather.23.cloned.1.call-start = ((), (), s32[]{:S(2)}) async-start(), calls=%async_computation.11 | async-start | bytes 15925248 | tf_op jit(solution)/shard_map/all_gather | solution.py:85
  335.9 420.1 %all-gather.25.cloned.1.call-start = ((), (), s32[]{:S(2)}) async-start(), calls=%async_computation.12 | async-start | bytes 15925248 | tf_op jit(solution)/shard_map/all_gather | solution.py:87
  336.6 753.9 %reduce-scatter.9.cloned.1.call-start = ((), (), s32[]{:S(2)}) async-start(), calls=%async_computation.14 | async-start | bytes 7077888 | tf_op jit(solution)/shard_map/reduce_scatter | solution.py:202
  337.3 29.1 %copy-start.44 = (f32[2]{0:T(128)}, f32[2]{0:T(128)S(1)}, u32[]{:S(2)}) copy-start(f32[2]{0:T(128)S(1)} %compare_convert_fusion) | copy-start | bytes 28
  349.7 456.7 %copy-start.33 = (f32[4608]{0:T(1024)}, f32[4608]{0:T(1024)S(1)}, u32[]{:S(2)}) copy-start(f32[4608]{0:T(1024)S(1)} %reshape.204) | copy-start | bytes 55300
  456.8 27.9 %copy-start.9 = (f32[2,16,512]{2,1,0:T(8,128)}, f32[2,16,512]{2,1,0:T(8,128)S(1)}, u32[]{:S(2)}) copy-start(f32[2,16,512]{2,1,0:T(8,128)S(1)} %log_add_fusion) | copy-start | bytes 196612
  499.6 2.8 copy-start
  499.6 3.6 copy-start.19
  500.2 142.3 %copy-start.27 = (f32[2,512]{1,0:T(2,128)}, f32[2,512]{1,0:T(2,128)S(1)}, u32[]{:S(2)}) copy-start(f32[2,512]{1,0:T(2,128)S(1)} %add_rsqrt_fusion) | copy-start | bytes 12292
  503.3 139.3 %copy-start.14 = (bf16[2,512,1152]{2,1,0:T(8,128)(2,1)}, bf16[2,512,1152]{2,1,0:T(8,128)(2,1)S(1)}, u32[]{:S(2)}) copy-start(bf16[2,512,1152]{2,1,0:T(8,128)(2,1)S(1)} %add_convert_fusion) | copy-start | bytes 7077892
  786.6 19.9 copy-start.41
  786.6 41.0 %slice-start = ((s8[4718592]{0:T(1024)(128)(4,1)}), s8[524288]{0:T(1024)(128)(4,1)S(1)}, s32[]{:S(2)}) async-start(s8[4718592]{0:T(1024)(128)(4,1)} %bitcast.93), calls=%async_computation.21 | async-start | bytes 1048576
  806.5 21.0 slice-start.1
  806.5 21.0 copy-start.4
  806.5 21.0 copy-start.6
  806.5 21.0 copy-start.20
  806.5 21.0 copy-start.26
  806.5 21.0 copy-start.28
  806.6 21.0 copy-start.45
  827.6 4.9 copy-start.24
  832.5 5.9 copy-start.50
  850.6 5.8 copy-start.10
  889.2 205.7 %reduce-scatter.7.cloned.1.call-start = ((), (), s32[]{:S(2)}) async-start(), calls=%async_computation.13 | async-start | bytes 7077888 | tf_op jit(solution)/shard_map/reduce_scatter | solution.py:199
  938.4 53.4 %copy-start.5 = (bf16[2,512,16,72]{1,3,2,0:T(8,128)(2,1)S(1)}, bf16[2,512,16,72]{1,3,2,0:T(8,128)(2,1)}, u32[]{:S(2)}) copy-start(bf16[2,512,16,72]{1,3,2,0:T(8,128)(2,1)} %copy.64) | copy-start | bytes 7077892
  1017.2 8.1 copy-start.34
  1017.2 100.8 %reduce-scatter.13.cloned.1.call-start = ((), (), s32[]{:S(2)}) async-start(), calls=%async_computation.16 | async-start | bytes 3981312 | tf_op jit(solution)/shard_map/reduce_scatter | solution.py:44
  1025.2 219.0 %reduce-scatter.17.cloned.1.call-start = ((), (), s32[]{:S(2)}) async-start(), calls=%async_computation.18 | async-start | bytes 15925248 | tf_op jit(solution)/shard_map/reduce_scatter | solution.py:44
  1048.8 321.5 %reduce-scatter.15.cloned.1.call-start = ((), (), s32[]{:S(2)}) async-start(), calls=%async_computation.17 | async-start | bytes 15925248 | tf_op jit(solution)/shard_map/reduce_scatter | solution.py:44
  1067.9 400.0 %reduce-scatter.11.cloned.1.call-start = ((), (), s32[]{:S(2)}) async-start(), calls=%async_computation.15 | async-start | bytes 11943936 | tf_op jit(solution)/shard_map/reduce_scatter | solution.py:44
  1090.5 8.7 copy-start.16
  1112.6 647.2 %all-reduce.12.cloned.1.call-start = ((), (), s32[]{:S(2)}) async-start(), calls=%async_computation.20 | async-start | bytes 31850496 | tf_op jit(solution)/shard_map/psum | solution.py:240
  1468.0 904.2 %all-gather.27.cloned.1.call-start = ((), (), s32[]{:S(2)}) async-start(), calls=%async_computation.19 | async-start | bytes 135364608 | tf_op jit(solution)/shard_map/all_gather | solution.py:236
  1468.6 18.1 copy-start.2
  1468.6 18.1 copy-start.22
  1468.6 18.1 copy-start.30
  1486.8 5.3 copy-start.3
  1492.1 6.4 copy-start.37
  1492.1 6.5 copy-start.36
  1492.1 6.5 copy-start.35
  1492.1 6.5 copy-start.38
  1492.1 6.5 copy-start.39
  1492.1 6.5 copy-start.40
  1492.1 14.1 copy-start.32
  1759.9 3.2 copy-start.11
  1759.9 7.8 slice-start.4
  1763.0 4.7 slice-start.5
  1763.0 13.1 slice-start.2
  1767.7 8.4 slice-start.3
  (8 other events, 13.3 us)
Sparse Core Ops, SparseCore 0:
  9.6 191.9 all-gather.12
  203.1 99.1 all-gather.14
  322.5 63.0 all-gather.18
  387.5 62.6 all-gather.16
  451.6 39.3 all-gather.20
  492.4 130.9 all-gather.22
  625.0 130.9 all-gather.24
  889.3 59.9 reduce-scatter.8
  1017.3 59.9 reduce-scatter.6
  1080.0 37.9 reduce-scatter.12
  1120.9 123.2 reduce-scatter.16
  1247.0 123.2 reduce-scatter.14
  1373.2 94.6 reduce-scatter.10
  1473.0 286.7 all-reduce.11
  1762.0 610.1 all-gather.26
